TPU v7x, 512 devices: a whole 4x4x16 slice. The times are simulated.
512 devices in a mesh: req: 128 (over y, z, core), tp: 4 (over x).
Axes of the slice: x: 4, y: 4, z: 16, core: 2. Of those that a mesh axis runs over, the one named last changes fastest.
Arguments:
- queries: bfloat16 [32768, 2048], P('req', 'tp'), may hold values from -160 to 160
- key_rows: bfloat16 [32768, 2048], P('req', 'tp'), may hold values from -6 to 6
- value_rows: bfloat16 [32768, 2048], P('req', 'tp'), may hold values from -6 to 6
- lengths: int32 [128, 4], P('req'), may hold values from 1 to 128, 256 in all within a row
- adapter_ids: int32 [128, 4], P('req'), may hold values from 0 to 127, as said below
- adapter_home: int32 [128], replicated, may hold values from 0 to 127, each once
- adapter_down: bfloat16 [128, 2048, 16], P('req', 'tp'), may hold values from -0.125 to 0.125
- adapter_up: bfloat16 [128, 16, 2048], P('req'), may hold values from -4 to 4
- output_weight: bfloat16 [2048, 2048], P('tp'), may hold values from -0.125 to 0.125
Outputs:
- block_output: bfloat16 [32768, 2048], P('req', 'tp')
Inputs may be any that keep to these rules, and one draw needn't show every extreme that they name: `adapter_ids`: all prompts together name exactly 16 distinct adapters.
All inputs are finite; a program needn't handle non-finite values.
Results may differ from a plain program's by a relative error of at most 0.0055.
Values may be sent and summed in bfloat16 or wider, within the bound.
A program may use at most 64 MiB of HBM per device.

v0:
```python
import math
import jax
import jax.numpy as jnp
from jax import lax
from jax.sharding import PartitionSpec as P

HD = 128


def segment_rows(length_row, row_total):
    boundary = jnp.cumsum(length_row)
    position = jnp.arange(row_total, dtype=jnp.int32)
    return jnp.sum((position[:, None] >= boundary[None, :]).astype(jnp.int32), axis=1)


def attend(queries, key_rows, value_rows, segment):
    row_total = queries.shape[0]
    head_count = queries.shape[1] // HD
    shaped_q = queries.reshape(row_total, head_count, HD)
    shaped_k = key_rows.reshape(row_total, head_count, HD)
    shaped_v = value_rows.reshape(row_total, head_count, HD)
    scores = jnp.einsum("qhd,khd->hqk", shaped_q, shaped_k, preferred_element_type=jnp.float32) * (
        1.0 / math.sqrt(HD)
    )
    position = jnp.arange(row_total, dtype=jnp.int32)
    allowed = (segment[:, None] == segment[None, :]) & (position[None, :] <= position[:, None])
    masked = jnp.where(allowed[None], scores, -1e30)
    highest = jnp.max(masked, axis=2, keepdims=True)
    exponent = jnp.where(allowed[None], jnp.exp(masked - highest), 0.0)
    weights = (exponent / jnp.sum(exponent, axis=2, keepdims=True)).astype(jnp.bfloat16)
    mixed = jnp.einsum("hqk,khd->qhd", weights, shaped_v, preferred_element_type=jnp.float32)
    return mixed.reshape(row_total, head_count * HD).astype(jnp.bfloat16)


def lowrank_delta(rank_rows, onehot, factor_up):
    row_total, prompts = onehot.shape
    rank_size = rank_rows.shape[1]
    spread = (onehot[:, :, None] * rank_rows[:, None, :]).reshape(row_total, prompts * rank_size)
    upper = factor_up.astype(jnp.float32).reshape(prompts * rank_size, factor_up.shape[2])
    return jnp.dot(spread, upper, precision=lax.Precision.HIGHEST)


def body(
    queries,
    key_rows,
    value_rows,
    lengths,
    adapter_ids,
    adapter_home,
    adapter_down,
    adapter_up,
    output_weight,
):
    row_total = queries.shape[0]
    prompts = lengths.shape[1]
    segment = segment_rows(lengths[0], row_total)
    prompt_ids = adapter_ids[0]
    downs_all, uppers_all = (
        lax.all_gather(adapter_down, "req", axis=0, tiled=True),
        lax.all_gather(adapter_up, "req", axis=0, tiled=True),
    )
    slot_rows = adapter_home[prompt_ids]
    downs = downs_all[slot_rows]
    uppers = uppers_all[slot_rows]
    attended = attend(queries, key_rows, value_rows, segment)
    onehot = (segment[:, None] == jnp.arange(prompts, dtype=jnp.int32)[None, :]).astype(jnp.float32)
    per_prompt = jnp.einsum("ta,sar->str", attended, downs, preferred_element_type=jnp.float32)
    low_local = jnp.einsum("ts,str->tr", onehot, per_prompt, precision=lax.Precision.HIGHEST)
    base_rows = jnp.dot(attended, output_weight, preferred_element_type=jnp.float32)
    partial_rows = base_rows + lowrank_delta(low_local, onehot, uppers)
    summed = lax.psum_scatter(partial_rows, "tp", scatter_dimension=1, tiled=True)
    return summed.astype(jnp.bfloat16)


def solution(mesh):
    return jax.shard_map(
        body,
        mesh=mesh,
        in_specs=(
            P("req", "tp"),
            P("req", "tp"),
            P("req", "tp"),
            P("req", None),
            P("req", None),
            P(),
            P("req", "tp", None),
            P("req", None, None),
            P("tp", None),
        ),
        out_specs=P("req", "tp"),
        check_vma=False,
    )
```

profile of v0, /device:TPU:1, one launch (start us, length us, event | category | flops | bytes accessed | tf_op | source)
XLA Modules:
  0.0 350.7 jit_solution(13716006195187594143)
XLA Ops:
  6.5 0.0 copy-start
  6.5 0.0 all-gather.3.cloned.1.call-start
  6.5 0.7 all-gather.3.cloned.1.call-update
  7.3 0.0 all-gather.5.cloned.1.call-start
  7.3 0.7 all-gather.5.cloned.1.call-update
  8.0 0.0 copy-start.1
  8.0 0.0 reduce-scatter.2.cloned.1.call-start
  8.1 1.8 copy.35
  9.9 0.7 fusion.20
  10.6 1.3 gather_fusion
  11.8 0.8 reduce-window.8
  12.7 0.1 convert_reduce_fusion
  12.8 0.1 fusion.11
  12.9 1.6 fusion.26
  14.5 0.0 copy-done.1
  14.5 1.3 fusion.4
  15.8 1.4 convolution_convert_fusion
  17.2 139.8 %all-gather.3.cloned.1.call-done = bf16[128,512,16]{1,2,0:T(8,128)(2,1)} async-done(((bf16[1,512,16]{1,2,0:T(8,128)(2,1)}), bf16[128,512,16]{1,2,0:T(8,128)(2,1)}) %all-gather.3.cloned.1.call-update) | async-done | bytes 2097168 | tf_op jit(solution)/shard_map/all_gather | solution.py:59
  157.0 2.1 gather_fusion.1
  159.1 0.2 fusion.6
  159.3 144.2 %all-gather.5.cloned.1.call-done = bf16[128,16,2048]{2,1,0:T(8,128)(2,1)} async-done(((bf16[1,16,2048]{2,1,0:T(8,128)(2,1)}), bf16[128,16,2048]{2,1,0:T(8,128)(2,1)}) %all-gather.5.cloned.1.call-update) | async-done | bytes 8388624 | tf_op jit(solution)/shard_map/all_gather | solution.py:60
  303.5 3.9 %gather_fusion.2 = bf16[4,16,2048]{2,1,0:T(8,128)(2,1)S(1)} fusion(bf16[128,16,2048]{2,1,0:T(8,128)(2,1)} %all-gather.5.cloned.1.call-done, s32[1024]{0:T(1024)S(1)} %pad_clamp_fusion), kind=kCustom, calls=%fused_computation.2 | custom fusion | bytes 524304 | tf_op jit(solution)/shard_map/gather | solution.py:64
  307.5 1.0 convolution_bitcast_fusion
  308.5 0.0 copy-done
  308.5 2.1 convolution_add_fusion
  310.6 0.0 reduce-scatter.2.cloned.1.call-update
  310.6 31.8 %reduce-scatter.2.cloned.1.call-done = f32[256,512]{1,0:T(8,128)} async-done(((f32[256,2048]{1,0:T(8,128)}), f32[256,512]{1,0:T(8,128)}) %reduce-scatter.2.cloned.1.call-update) | async-done | bytes 524304 | tf_op jit(solution)/shard_map/reduce_scatter | solution.py:71
  342.4 1.8 convert_element_type.32
  (4 shorter events, 0.0 us)
Async XLA Ops:
  6.5 302.0 %copy-start = (bf16[512,2048]{1,0:T(8,128)(2,1)S(1)}, bf16[512,2048]{1,0:T(8,128)(2,1)}, u32[]{:S(2)}) copy-start(bf16[512,2048]{1,0:T(8,128)(2,1)} %param.17) | copy-start | bytes 6291460
  6.5 150.4 %all-gather.3.cloned.1.call-start = ((), (), s32[]{:S(2)}) async-start(), calls=%async_computation.1 | async-start | bytes 2113536 | tf_op jit(solution)/shard_map/all_gather | solution.py:59
  7.3 296.3 %all-gather.5.cloned.1.call-start = ((), (), s32[]{:S(2)}) async-start(), calls=%async_computation.2 | async-start | bytes 8454144 | tf_op jit(solution)/shard_map/all_gather | solution.py:60
  8.0 6.5 %copy-start.1 = (bf16[256,512]{1,0:T(8,128)(2,1)S(1)}, bf16[256,512]{1,0:T(8,128)(2,1)}, u32[]{:S(2)}) copy-start(bf16[256,512]{1,0:T(8,128)(2,1)} %param.10) | copy-start | bytes 786436
  8.0 334.4 %reduce-scatter.2.cloned.1.call-start = ((), (), s32[]{:S(2)}) async-start(), calls=%async_computation.3 | async-start | bytes 2621440 | tf_op jit(solution)/shard_map/reduce_scatter | solution.py:71
Sparse Core Ops, SparseCore 0:
  10.5 146.4 all-gather.2
  160.1 143.3 all-gather.4
  310.8 31.6 reduce-scatter.1
where the time goes:
time: 351 us
  waiting for transfers between devices  317 us (90%)
  between operations  13.2 us (4%)
  local copies, waits for them, and re-layouts  9.21 us (3%)
  matrix products  7.58 us (2%)
    all_gather x1, waiting for transfers between devices, body(): lax.all_gather(adapter_up, 'req', axis=0, tiled=True)  144 us
    all_gather x1, waiting for transfers between devices, body(): lax.all_gather(adapter_down, 'req', axis=0, tiled=True)  140 us
    reduce_scatter x1, waiting for transfers between devices, body(): lax.psum_scatter(partial_rows, 'tp', scatter_dimension=1, tiled=True)  31.8 us
  transfers between devices with their start and end apart: 3, of which 3 were waited for; matrix products, arithmetic and copies ran while one was open for 3% of the time, Pallas kernels for 0%

commit v1 on v0

--- a/solution.py
+++ b/solution.py
@@ -1,3 +1,4 @@
+import functools
 import math
 import jax
 import jax.numpy as jnp
@@ -5,6 +6,14 @@
 from jax.sharding import PartitionSpec as P
 
 HD = 128
+
+
+def _wait_arrays(base_x, peer_axis):
+    high = lax.all_to_all(jnp.stack(lax.axis_size(peer_axis) * [base_x]), peer_axis, 0, 0)
+    return jnp.concatenate(high, axis=0)
+
+
+play_digits_on_mesh = functools.partial(_wait_arrays, peer_axis="req")
 
 
 def segment_rows(length_row, row_total):
@@ -56,7 +65,7 @@
     segment = segment_rows(lengths[0], row_total)
     prompt_ids = adapter_ids[0]
     downs_all, uppers_all = (
-        lax.all_gather(adapter_down, "req", axis=0, tiled=True),
+        play_digits_on_mesh(adapter_down),
         lax.all_gather(adapter_up, "req", axis=0, tiled=True),
     )
     slot_rows = adapter_home[prompt_ids]

time: 351 us -> 227 us (0.65)
  waiting for transfers between devices: 317 us -> 173 us
  starting transfers between devices: 0.08 us -> 21.2 us
    all_gather x1 -> x0, waiting for transfers between devices: 140 us -> none  [body(): lax.all_gather(adapter_down, 'req', axis=0, tiled=True)]
    all_gather x1, waiting for transfers between devices: 144 us -> 36.4 us  [body(): lax.all_gather(adapter_up, 'req', axis=0, tiled=True)]
    all_to_all x0 -> x1, waiting for transfers between devices: none -> 102 us  [_wait_arrays(): lax.all_to_all(jnp.stack(lax.axis_size(peer_axis) * [base_x]), peer_axis,...]
    all_to_all x0 -> x1, starting transfers between devices: none -> 21.2 us  [_wait_arrays(): lax.all_to_all(jnp.stack(lax.axis_size(peer_axis) * [base_x]), peer_axis,...]
  transfers between devices with their start and end apart: 3 -> 3, of which waited for: 3 -> 3; matrix products, arithmetic and copies ran while one was open for 3% -> 4% of each run, Pallas kernels for 0% -> 0%
where the time goes in v1:
time: 227 us; the launch traced here: 226 us
  waiting for transfers between devices  173 us (76%)
  starting transfers between devices  21.2 us (9%)
  between operations  13.5 us (6%)
  local copies, waits for them, and re-layouts  9.94 us (4%)
  matrix products  6.65 us (3%)
    all_to_all x1, waiting for transfers between devices, _wait_arrays(): lax.all_to_all(jnp.stack(lax.axis_size(peer_axis) * [base_x]), peer_axis,...  102 us
    all_gather x1, waiting for transfers between devices, body(): lax.all_gather(adapter_up, 'req', axis=0, tiled=True)  36.4 us
    reduce_scatter x1, waiting for transfers between devices, body(): lax.psum_scatter(partial_rows, 'tp', scatter_dimension=1, tiled=True)  33.8 us
    all_to_all x1, starting transfers between devices, _wait_arrays(): lax.all_to_all(jnp.stack(lax.axis_size(peer_axis) * [base_x]), peer_axis,...  21.2 us
  transfers between devices with their start and end apart: 3, of which 3 were waited for; matrix products, arithmetic and copies ran while one was open for 4% of the time, Pallas kernels for 0%

profile of v1, /device:TPU:1, one launch (start us, length us, event | category | flops | bytes accessed | tf_op | source)
XLA Modules:
  0.0 226.4 jit_solution(15551247581610302231)
XLA Ops:
  6.5 0.0 copy-start
  6.5 0.0 all-gather.2.cloned.1.call-start
  6.5 0.7 all-gather.2.cloned.1.call-update
  7.3 2.3 %stack.2 = bf16[128,1,512,16]{2,3,1,0:T(8,128)(2,1)} broadcast(bf16[512,16]{0,1:T(8,128)(2,1)} %bitcast.68), dimensions={2,3} | broadcast | bytes 2113536 | tf_op jit(solution)/shard_map/stack | solution.py:12
  9.5 0.0 copy-start.4
  9.5 0.0 copy-start.5
  9.5 0.0 copy-start.1
  9.5 0.0 copy-start.6
  9.5 0.0 copy-start.2
  9.6 0.0 copy-start.3
  9.6 21.2 %all-to-all-start = ((bf16[128,1,512,16]{2,3,1,0:T(8,128)(2,1)}), bf16[128,1,512,16]{2,3,1,0:T(8,128)(2,1)}, u32[]{:S(2)}, u32[]{:S(2)}) async-start(bf16[128,1,512,16]{2,3,1,0:T(8,128)(2,1)} %stack.2), calls=%async_computation | async-start | bytes 4194304 | tf_op jit(solution)/shard_map/all_to_all | solution.py:12
  30.7 0.0 reduce-scatter.2.cloned.1.call-start
  30.8 0.0 copy-done.4
  30.8 0.8 copy.37
  31.6 0.0 copy-done.5
  31.6 0.0 copy-done.1
  31.7 0.6 gather_fusion
  32.3 0.0 copy-done.6
  32.3 0.2 reduce-window.8
  32.5 0.1 convert_reduce_fusion
  32.6 0.1 fusion.11
  32.7 0.0 copy-done.2
  32.7 0.0 copy-done.3
  32.7 0.6 fusion.26
  33.3 1.3 fusion.4
  34.6 1.4 convolution_convert_fusion
  36.1 101.9 %all-to-all-done = bf16[128,1,512,16]{2,3,1,0:T(8,128)(2,1)} async-done(((bf16[128,1,512,16]{2,3,1,0:T(8,128)(2,1)}), bf16[128,1,512,16]{2,3,1,0:T(8,128)(2,1)}, u32[]{:S(2)}, u32[]{:S(2)}) %all-to-all-start) | async-done | bytes 2097184 | tf_op jit(solution)/shard_map/all_to_all | solution.py:12
  138.0 2.2 gather_fusion.1
  140.2 0.2 fusion.6
  140.4 36.4 %all-gather.2.cloned.1.call-done = bf16[128,16,2048]{2,1,0:T(8,128)(2,1)} async-done(((bf16[1,16,2048]{2,1,0:T(8,128)(2,1)}), bf16[128,16,2048]{2,1,0:T(8,128)(2,1)}) %all-gather.2.cloned.1.call-update) | async-done | bytes 8388624 | tf_op jit(solution)/shard_map/all_gather | solution.py:69
  176.8 3.9 %gather_fusion.2 = bf16[4,16,2048]{2,1,0:T(8,128)(2,1)S(1)} fusion(bf16[128,16,2048]{2,1,0:T(8,128)(2,1)} %all-gather.2.cloned.1.call-done, s32[1024]{0:T(1024)S(1)} %pad_clamp_fusion), kind=kCustom, calls=%fused_computation.2 | custom fusion | bytes 524304 | tf_op jit(solution)/shard_map/gather | solution.py:73
  180.7 1.0 convolution_bitcast_fusion
  181.8 0.0 copy-done
  181.8 2.1 convolution_add_fusion
  183.9 0.0 reduce-scatter.2.cloned.1.call-update
  183.9 33.8 %reduce-scatter.2.cloned.1.call-done = f32[256,512]{1,0:T(8,128)} async-done(((f32[256,2048]{1,0:T(8,128)}), f32[256,512]{1,0:T(8,128)}) %reduce-scatter.2.cloned.1.call-update) | async-done | bytes 524304 | tf_op jit(solution)/shard_map/reduce_scatter | solution.py:80
  217.7 1.8 convert_element_type.32
  (5 shorter events, 0.0 us)
Async XLA Ops:
  6.5 175.2 %copy-start = (bf16[512,2048]{1,0:T(8,128)(2,1)S(1)}, bf16[512,2048]{1,0:T(8,128)(2,1)}, u32[]{:S(2)}) copy-start(bf16[512,2048]{1,0:T(8,128)(2,1)} %param.17) | copy-start | bytes 6291460
  6.5 170.2 %all-gather.2.cloned.1.call-start = ((), (), s32[]{:S(2)}) async-start(), calls=%async_computation.2 | async-start | bytes 8454144 | tf_op jit(solution)/shard_map/all_gather | solution.py:69
  9.5 21.2 %copy-start.4 = (bf16[256,512]{1,0:T(8,128)(2,1)S(1)}, bf16[256,512]{1,0:T(8,128)(2,1)}, u32[]{:S(2)}) copy-start(bf16[256,512]{1,0:T(8,128)(2,1)} %param.11) | copy-start | bytes 786436
  9.5 22.1 %copy-start.5 = (s32[1,4]{1,0:T(1,128)S(1)}, s32[1,4]{1,0:T(1,128)}, u32[]{:S(2)}) copy-start(s32[1,4]{1,0:T(1,128)} %param.13) | copy-start | bytes 52
  9.5 22.1 %copy-start.1 = (s32[128]{0:T(128)S(1)}, s32[128]{0:T(128)}, u32[]{:S(2)}) copy-start(s32[128]{0:T(128)} %param.14) | copy-start | bytes 1540
  9.5 22.8 %copy-start.6 = (s32[1,4]{1,0:T(1,128)S(1)}, s32[1,4]{1,0:T(1,128)}, u32[]{:S(2)}) copy-start(s32[1,4]{1,0:T(1,128)} %param.12) | copy-start | bytes 52
  9.5 23.1 %copy-start.2 = (bf16[256,512]{1,0:T(8,128)(2,1)S(1)}, bf16[256,512]{1,0:T(8,128)(2,1)}, u32[]{:S(2)}) copy-start(bf16[256,512]{1,0:T(8,128)(2,1)} %param.10) | copy-start | bytes 786436
  9.6 23.1 %copy-start.3 = (bf16[256,512]{1,0:T(8,128)(2,1)S(1)}, bf16[256,512]{1,0:T(8,128)(2,1)}, u32[]{:S(2)}) copy-start(bf16[256,512]{1,0:T(8,128)(2,1)} %param.9) | copy-start | bytes 786436
  9.6 128.4 %all-to-all-start = ((bf16[128,1,512,16]{2,3,1,0:T(8,128)(2,1)}), bf16[128,1,512,16]{2,3,1,0:T(8,128)(2,1)}, u32[]{:S(2)}, u32[]{:S(2)}) async-start(bf16[128,1,512,16]{2,3,1,0:T(8,128)(2,1)} %stack.2), calls=%async_computation | async-start | bytes 4194304 | tf_op jit(solution)/shard_map/all_to_all | solution.py:12
  30.7 187.0 %reduce-scatter.2.cloned.1.call-start = ((), (), s32[]{:S(2)}) async-start(), calls=%async_computation.3 | async-start | bytes 2621440 | tf_op jit(solution)/shard_map/reduce_scatter | solution.py:80
Sparse Core Ops, SparseCore 0:
  10.5 166.2 all-gather.1
  184.0 33.6 reduce-scatter.1
